TPU v7x, 256 devices: a whole 4x4x8 slice. The times are simulated.
256 devices in a mesh: seq: 16 (over x, y_hi, core), fsdp: 16 (over z, y_lo).
Axes of the slice: x: 4, y: 4 (y_hi: 2, y_lo: 2; y = y_hi * 2 + y_lo), z: 8, core: 2. Of those that a mesh axis runs over, the one named last changes fastest.
Arguments:
- hidden: bfloat16 [32768, 8192], P(('seq', 'fsdp')), may hold values from -24 to 24
- kv_blocks: bfloat16 [8192, 1024], P('fsdp'), may hold values from -0.0625 to 0.0625
- kv_scale: float32 [64, 8], P('fsdp'), may hold values from 0.5 to 2
- queries: bfloat16 [32768, 4096], P(('seq', 'fsdp')), may hold values from -24 to 24
- grad_out: bfloat16 [32768, 4096], P(('seq', 'fsdp')), may hold values from -6 to 6
Outputs:
- attn_out: bfloat16 [32768, 4096], P(('seq', 'fsdp'))
- grad_queries: bfloat16 [32768, 4096], P(('seq', 'fsdp'))
- grad_hidden: bfloat16 [32768, 8192], P(('seq', 'fsdp'))
- weight_grad: float32 [8192, 1024], P('fsdp')
All inputs are finite; a program needn't handle non-finite values.
Results may differ from a plain program's by a relative error of at most 0.0075.
The roundings to bfloat16 on the way count: a program that leaves them out, or rounds other values in their place, can miss the bound.
Values may be sent and summed in bfloat16 or wider, within the bound.
No kernel may reach another device: no remote copies, remote signals or barrier semaphores. Data moves between devices by JAX's collectives and lax.ppermute only.
A program may use at most 128 MiB of HBM per device.

v0:
```python
import jax
import jax.numpy as jnp
from jax import lax
from jax.sharding import Mesh
from jax.sharding import PartitionSpec as P

HEADS = 32
KV_HEADS = 4
HEAD = 128
QB = 128
FSDP = ("fsdp_0", "fsdp_1")
SEQ_FSDP = ("seq", "fsdp_0", "fsdp_1")
NEG = -1e30


def gather_axes(value, axes, dim):
    if not axes:
        return value
    nearer = lax.all_gather(value, axes[-1], axis=dim, tiled=True)
    return gather_axes(nearer, axes[:-1], dim)


def shifted(block, axis, distance):
    devices = range(lax.axis_size(axis))
    route = [(i - distance, i) for i in devices if i - distance in devices]
    return lax.ppermute(block, axis, route)


def dequantize(blocks, scale):
    rows, cols = blocks.shape
    grid = blocks.astype(jnp.float32).reshape(scale.shape[0], QB, scale.shape[1], QB)
    return (grid * scale[:, None, :, None]).reshape(rows, cols).astype(jnp.bfloat16)


def attend_group(operands, allowed):
    qgrp, kgrp, vgrp, ggrp = operands
    factor = 1.0 / float(HEAD) ** 0.5
    scores = jnp.einsum("rhd,kd->rhk", qgrp, kgrp, preferred_element_type=jnp.float32) * factor
    scores = jnp.where(allowed[:, None, :], scores, NEG)
    top = jnp.max(scores, axis=-1, keepdims=True)
    expd = jnp.exp(scores - top)
    probs = expd / jnp.sum(expd, axis=-1, keepdims=True)
    probs_b = probs.astype(jnp.bfloat16)
    output = jnp.einsum("rhk,kd->rhd", probs_b, vgrp, preferred_element_type=jnp.float32).astype(
        jnp.bfloat16
    )
    dprobs = jnp.einsum("rhd,kd->rhk", ggrp, vgrp, preferred_element_type=jnp.float32)
    delta = jnp.sum(probs * dprobs, axis=-1, keepdims=True)
    dscores = (probs * (dprobs - delta) * factor).astype(jnp.bfloat16)
    gradq = jnp.einsum("rhk,kd->rhd", dscores, kgrp, preferred_element_type=jnp.float32).astype(
        jnp.bfloat16
    )
    gradk = jnp.einsum("rhk,rhd->kd", dscores, qgrp, preferred_element_type=jnp.float32)
    gradv = jnp.einsum("rhk,rhd->kd", probs_b, ggrp, preferred_element_type=jnp.float32)
    return (output, gradq, gradk, gradv)


def attend(queries, window, grad_out, allowed):
    rows = queries.shape[0]
    count = window.shape[0]
    group = HEADS // KV_HEADS
    kvw = KV_HEADS * HEAD
    qgrp = queries.reshape(rows, KV_HEADS, group, HEAD).transpose(1, 0, 2, 3)
    ggrp = grad_out.reshape(rows, KV_HEADS, group, HEAD).transpose(1, 0, 2, 3)
    kgrp = window[:, :kvw].reshape(count, KV_HEADS, HEAD).transpose(1, 0, 2)
    vgrp = window[:, kvw:].reshape(count, KV_HEADS, HEAD).transpose(1, 0, 2)
    output, gradq, gradk, gradv = lax.map(
        lambda ops: attend_group(ops, allowed), (qgrp, kgrp, vgrp, ggrp)
    )
    output = output.transpose(1, 0, 2, 3).reshape(rows, HEADS * HEAD)
    gradq = gradq.transpose(1, 0, 2, 3).reshape(rows, HEADS * HEAD)
    gradk = gradk.transpose(1, 0, 2).reshape(count, kvw)
    gradv = gradv.transpose(1, 0, 2).reshape(count, kvw)
    return (output, gradq, jnp.concatenate([gradk, gradv], axis=1))


def body(hidden, kv_blocks, kv_scale, queries, grad_out):
    tok = hidden.shape[0]
    groups = lax.axis_size(FSDP)
    reach = groups // 2
    place = lax.axis_index(FSDP)
    linear = lax.axis_index("seq") * groups + place
    weights = dequantize(kv_blocks, kv_scale)
    columns = lax.all_to_all(hidden, FSDP, split_axis=1, concat_axis=0, tiled=True)
    whole = gather_axes(weights, FSDP, 0)
    kv = jnp.dot(hidden, whole, preferred_element_type=jnp.float32).astype(jnp.bfloat16)
    pieces = []
    for offset in range(reach, 0, -1):
        pieces.append(shifted(kv, SEQ_FSDP, offset))
    window = jnp.concatenate(pieces + [kv], axis=0)
    base = linear * tok
    qpos = base + jnp.arange(tok, dtype=jnp.int32)
    kpos = base - reach * tok + jnp.arange((reach + 1) * tok, dtype=jnp.int32)
    span = reach * tok
    allowed = (
        (qpos[:, None] - kpos[None, :] < span)
        & (kpos[None, :] <= qpos[:, None])
        & (kpos[None, :] >= 0)
    )
    attn_out, grad_queries, dwin = attend(queries, window, grad_out, allowed)
    total = dwin[reach * tok :]
    inside = total
    for offset in range(1, reach + 1):
        piece = dwin[(reach - offset) * tok : (reach - offset + 1) * tok]
        returned = shifted(piece, SEQ_FSDP, -offset)
        total = total + returned
        inside = inside + jnp.where(place + offset < groups, returned, jnp.zeros_like(returned))
    all_grad = total.astype(jnp.bfloat16)
    seg_grad = inside.astype(jnp.bfloat16)
    grad_hidden = lax.dot_general(
        seg_grad, whole, (((1,), (1,)), ((), ())), preferred_element_type=jnp.float32
    ).astype(jnp.bfloat16)
    shard_grad = lax.dot_general(
        columns,
        lax.all_gather(all_grad, FSDP, axis=0, tiled=True),
        (((0,), (0,)), ((), ())),
        preferred_element_type=jnp.float32,
    )
    weight_grad = lax.psum(shard_grad, "seq")
    return (attn_out, grad_queries, grad_hidden, weight_grad)


def solution(mesh):
    finer = Mesh(mesh.devices.reshape(mesh.shape["seq"], 8, 2), ("seq", "fsdp_0", "fsdp_1"))
    placed = (P(SEQ_FSDP, None), P(FSDP, None), P(FSDP, None), P(SEQ_FSDP, None), P(SEQ_FSDP, None))
    return jax.shard_map(
        body,
        mesh=finer,
        in_specs=placed,
        out_specs=(P(SEQ_FSDP, None), P(SEQ_FSDP, None), P(SEQ_FSDP, None), P(FSDP, None)),
        check_vma=False,
    )
```

profile of v0, /device:TPU:1, one launch (start us, length us, event | category | flops | bytes accessed | tf_op | source)
XLA Modules:
  0.0 1012.2 jit_solution(2476808071577137936)
XLA Ops:
  10.0 42.4 %all-gather.4.cloned.1.call-done = bf16[1024,1024]{1,0:T(8,128)(2,1)} async-done(((bf16[512,1024]{1,0:T(8,128)(2,1)}), bf16[1024,1024]{1,0:T(8,128)(2,1)}) %all-gather.4.cloned.1.call-update) | async-done | bytes 2097168 | tf_op jit(solution)/shard_map/all_gather | solution.py:19
  52.5 175.5 %all-gather.6.cloned.1.call-done = bf16[8192,1024]{1,0:T(8,128)(2,1)} async-done(((bf16[1024,1024]{1,0:T(8,128)(2,1)}), bf16[8192,1024]{1,0:T(8,128)(2,1)}) %all-gather.6.cloned.1.call-update) | async-done | bytes 16777232 | tf_op jit(solution)/shard_map/all_gather | solution.py:19
  271.7 18.8 %collective-permute-done.2 = bf16[128,1024]{1,0:T(8,128)(2,1)S(1)} collective-permute-done((bf16[128,1024]{1,0:T(8,128)(2,1)S(1)}, bf16[128,1024]{1,0:T(8,128)(2,1)S(1)}, u32[]{:S(2)}, u32[]{:S(2)}) %collective-permute-start.2) | collective-permute-done | bytes 262176 | tf_op jit(solution)/shard_map/ppermute | solution.py:26
  292.5 13.1 %collective-permute-done.3 = bf16[128,1024]{1,0:T(8,128)(2,1)S(1)} collective-permute-done((bf16[128,1024]{1,0:T(8,128)(2,1)S(1)}, bf16[128,1024]{1,0:T(8,128)(2,1)S(1)}, u32[]{:S(2)}, u32[]{:S(2)}) %collective-permute-start.3) | collective-permute-done | bytes 262176 | tf_op jit(solution)/shard_map/ppermute | solution.py:26
  313.4 8.5 collective-permute-done.6
  321.9 12.2 %collective-permute-done.7 = bf16[128,1024]{1,0:T(8,128)(2,1)S(1)} collective-permute-done((bf16[128,1024]{1,0:T(8,128)(2,1)S(1)}, bf16[128,1024]{1,0:T(8,128)(2,1)S(1)}, u32[]{:S(2)}, u32[]{:S(2)}) %collective-permute-start.7) | collective-permute-done | bytes 262176 | tf_op jit(solution)/shard_map/ppermute | solution.py:26
  336.1 180.6 %while.17 = (s32[]{:T(128)}, bf16[4,128,8,128]{3,1,2,0:T(8,128)(2,1)}, bf16[4,128,8,128]{3,1,2,0:T(8,128)(2,1)}, f32[4,1152,128]{1,2,0:T(8,128)S(1)}, f32[4,1152...) while((s32[]{:T(128)}, ...), condition=%wide.region_4.5_spmd.clone, body=%wide.region_0.4_spmd.clone.sunk | while | flops 2449958400 | bytes 52865276 | solution.py:67
  346.7 12.1 %fusion.171 = f32[4,1152,128]{1,2,0:T(8,128)S(1)} fusion(f32[4,1152,128]{1,2,0:T(8,128)S(1)} %get-tuple-element.259, s32[]{:T(128)} %get-tuple-element.256, f32[128,8,1152]{2,0,1:T(8,128)} %fusion.169, bf16[4,128,8,128]{1,3,2,0:T(8,128)(2,1)} %get-tuple-element.274, f32[128,8,1152]{2,0,1:T(8,128)} %get-tuple-element.242, ...), kind=kOutput, calls=%fused_computation.17.clone.1 | convolution fusion | flops 310249600 | bytes 19735552 | tf_op jit(solution)/shard_map/while/body/eval_jaxpr/rhk,rhd->kd/dot_general | solution.py:53
  358.7 12.5 %fusion.170 = bf16[4,128,8,128]{3,1,2,0:T(8,128)(2,1)} fusion(bf16[4,128,8,128]{3,1,2,0:T(8,128)(2,1)} %get-tuple-element.258, s32[]{:T(128)} %get-tuple-element.256, f32[128,8,1152]{2,0,1:T(8,128)} %fusion.169, bf16[4,1152,128]{2,1,0:T(8,128)(2,1)} %get-tuple-element.275, f32[128,8,1152]{2,0,1:T(8,128)} %get-tuple-element.242, ...), kind=kOutput, calls=%fused_computation.28.clone.1 | convolution fusion | flops 310380672 | bytes 19440640 | tf_op jit(solution)/shard_map/while/body/eval_jaxpr/rhk,kd->rhd/dot_general | solution.py:50
  391.8 12.1 %fusion.171 = f32[4,1152,128]{1,2,0:T(8,128)S(1)} fusion(f32[4,1152,128]{1,2,0:T(8,128)S(1)} %get-tuple-element.259, s32[]{:T(128)} %get-tuple-element.256, f32[128,8,1152]{2,0,1:T(8,128)} %fusion.169, bf16[4,128,8,128]{1,3,2,0:T(8,128)(2,1)} %get-tuple-element.274, f32[128,8,1152]{2,0,1:T(8,128)} %get-tuple-element.242, ...), kind=kOutput, calls=%fused_computation.17.clone.1 | convolution fusion | flops 310249600 | bytes 19735552 | tf_op jit(solution)/shard_map/while/body/eval_jaxpr/rhk,rhd->kd/dot_general | solution.py:53
  403.9 12.5 %fusion.170 = bf16[4,128,8,128]{3,1,2,0:T(8,128)(2,1)} fusion(bf16[4,128,8,128]{3,1,2,0:T(8,128)(2,1)} %get-tuple-element.258, s32[]{:T(128)} %get-tuple-element.256, f32[128,8,1152]{2,0,1:T(8,128)} %fusion.169, bf16[4,1152,128]{2,1,0:T(8,128)(2,1)} %get-tuple-element.275, f32[128,8,1152]{2,0,1:T(8,128)} %get-tuple-element.242, ...), kind=kOutput, calls=%fused_computation.28.clone.1 | convolution fusion | flops 310380672 | bytes 19440640 | tf_op jit(solution)/shard_map/while/body/eval_jaxpr/rhk,kd->rhd/dot_general | solution.py:50
  437.0 12.1 %fusion.171 = f32[4,1152,128]{1,2,0:T(8,128)S(1)} fusion(f32[4,1152,128]{1,2,0:T(8,128)S(1)} %get-tuple-element.259, s32[]{:T(128)} %get-tuple-element.256, f32[128,8,1152]{2,0,1:T(8,128)} %fusion.169, bf16[4,128,8,128]{1,3,2,0:T(8,128)(2,1)} %get-tuple-element.274, f32[128,8,1152]{2,0,1:T(8,128)} %get-tuple-element.242, ...), kind=kOutput, calls=%fused_computation.17.clone.1 | convolution fusion | flops 310249600 | bytes 19735552 | tf_op jit(solution)/shard_map/while/body/eval_jaxpr/rhk,rhd->kd/dot_general | solution.py:53
  449.0 12.5 %fusion.170 = bf16[4,128,8,128]{3,1,2,0:T(8,128)(2,1)} fusion(bf16[4,128,8,128]{3,1,2,0:T(8,128)(2,1)} %get-tuple-element.258, s32[]{:T(128)} %get-tuple-element.256, f32[128,8,1152]{2,0,1:T(8,128)} %fusion.169, bf16[4,1152,128]{2,1,0:T(8,128)(2,1)} %get-tuple-element.275, f32[128,8,1152]{2,0,1:T(8,128)} %get-tuple-element.242, ...), kind=kOutput, calls=%fused_computation.28.clone.1 | convolution fusion | flops 310380672 | bytes 19440640 | tf_op jit(solution)/shard_map/while/body/eval_jaxpr/rhk,kd->rhd/dot_general | solution.py:50
  482.1 12.1 %fusion.171 = f32[4,1152,128]{1,2,0:T(8,128)S(1)} fusion(f32[4,1152,128]{1,2,0:T(8,128)S(1)} %get-tuple-element.259, s32[]{:T(128)} %get-tuple-element.256, f32[128,8,1152]{2,0,1:T(8,128)} %fusion.169, bf16[4,128,8,128]{1,3,2,0:T(8,128)(2,1)} %get-tuple-element.274, f32[128,8,1152]{2,0,1:T(8,128)} %get-tuple-element.242, ...), kind=kOutput, calls=%fused_computation.17.clone.1 | convolution fusion | flops 310249600 | bytes 19735552 | tf_op jit(solution)/shard_map/while/body/eval_jaxpr/rhk,rhd->kd/dot_general | solution.py:53
  494.2 12.5 %fusion.170 = bf16[4,128,8,128]{3,1,2,0:T(8,128)(2,1)} fusion(bf16[4,128,8,128]{3,1,2,0:T(8,128)(2,1)} %get-tuple-element.258, s32[]{:T(128)} %get-tuple-element.256, f32[128,8,1152]{2,0,1:T(8,128)} %fusion.169, bf16[4,1152,128]{2,1,0:T(8,128)(2,1)} %get-tuple-element.275, f32[128,8,1152]{2,0,1:T(8,128)} %get-tuple-element.242, ...), kind=kOutput, calls=%fused_computation.28.clone.1 | convolution fusion | flops 310380672 | bytes 19440640 | tf_op jit(solution)/shard_map/while/body/eval_jaxpr/rhk,kd->rhd/dot_general | solution.py:50
  536.8 17.9 %collective-permute-start.15 = (f32[128,1024]{0,1:T(8,128)S(1)}, f32[128,1024]{0,1:T(8,128)S(1)}, u32[]{:S(2)}, u32[]{:S(2)}) collective-permute-start(f32[128,1024]{0,1:T(8,128)S(1)} %get-tuple-element.160), channel_id=1, source_target_pairs={{8,0},{9,1},{10,2},{11,3},{12,4},{13,5},{14,6},{15,7},{16,8},{17,9... | collective-permute-start | bytes 1572872 | tf_op jit(solution)/shard_map/ppermute | solution.py:26
  554.7 15.7 %collective-permute-done.11 = f32[128,1024]{0,1:T(8,128)S(1)} collective-permute-done((f32[128,1024]{0,1:T(8,128)S(1)}, f32[128,1024]{0,1:T(8,128)S(1)}, u32[]{:S(2)}, u32[]{:S(2)}) %collective-permute-start.11) | collective-permute-done | bytes 524320 | tf_op jit(solution)/shard_map/ppermute | solution.py:26
  570.5 17.8 %collective-permute-start.8 = (f32[128,1024]{0,1:T(8,128)S(1)}, f32[128,1024]{0,1:T(8,128)S(1)}, u32[]{:S(2)}, u32[]{:S(2)}) collective-permute-start(f32[128,1024]{0,1:T(8,128)S(1)} %get-tuple-element.154), channel_id=1, source_target_pairs={{1,0},{2,1},{3,2},{4,3},{5,4},{6,5},{7,6},{8,7},{9,8},{10,9},{11,1... | collective-permute-start | bytes 1572872 | tf_op jit(solution)/shard_map/ppermute | solution.py:26
  588.3 13.7 %collective-permute-start.9 = (f32[128,1024]{0,1:T(8,128)S(1)}, f32[128,1024]{0,1:T(8,128)S(1)}, u32[]{:S(2)}, u32[]{:S(2)}) collective-permute-start(f32[128,1024]{0,1:T(8,128)S(1)} %get-tuple-element.155), channel_id=1, source_target_pairs={{2,0},{3,1},{4,2},{5,3},{6,4},{7,5},{8,6},{9,7},{10,8},{11,9},{12,... | collective-permute-start | bytes 1572872 | tf_op jit(solution)/shard_map/ppermute | solution.py:26
  602.0 32.7 %collective-permute-done.13 = f32[128,1024]{0,1:T(8,128)S(1)} collective-permute-done((f32[128,1024]{0,1:T(8,128)S(1)}, f32[128,1024]{0,1:T(8,128)S(1)}, u32[]{:S(2)}, u32[]{:S(2)}) %collective-permute-start.13) | collective-permute-done | bytes 524320 | tf_op jit(solution)/shard_map/ppermute | solution.py:26
  649.5 131.0 %all_to_all.19 = bf16[128,16,512]{0,2,1:T(8,128)(2,1)} all-to-all(bf16[128,16,512]{0,2,1:T(8,128)(2,1)} %bitcast.168), channel_id=1, replica_groups=mesh['seq'=16,'fsdp_0'=8,'fsdp_1'=2] {'fsdp_0','fsdp_1'}, dimensions={1} | all-to-all | bytes 4194304 | tf_op jit(solution)/shard_map/all_to_all | solution.py:84
  784.4 56.0 %all-gather.8.cloned.1.call-done = bf16[2048,1024]{0,1:T(8,128)(2,1)} async-done(((bf16[128,1024]{0,1:T(8,128)(2,1)}), bf16[2048,1024]{0,1:T(8,128)(2,1)}) %all-gather.8.cloned.1.call-update) | async-done | bytes 4194320 | tf_op jit(solution)/shard_map/all_gather | solution.py:115
  852.6 13.9 %convolution_convert_fusion.1 = bf16[128,8192]{1,0:T(8,128)(2,1)} fusion(bf16[8192,1024]{1,0:T(8,128)(2,1)} %all-gather.6.cloned.1.call-done, f32[128,1024]{0,1:T(8,128)} %copy-done.5, f32[128,1024]{0,1:T(8,128)} %copy-done.4, f32[128,1024]{0,1:T(8,128)} %copy-done.3, f32[128,1024]{0,1:T(8,128)} %copy-done.2, f32[128,1024]{0,1:T(8,128)S(1)} %collective-permute-done.11, ...), kind=kOutput, calls=%fused_computation.83 | convolution fusion | flops 2150891520 | bytes 27787272 | tf_op jit(solution)/shard_map/dot_general | solution.py:110
  866.5 136.3 %all-reduce.2.cloned.1.call-done = f32[512,1024]{0,1:T(8,128)} async-done(((f32[512,1024]{0,1:T(8,128)}), f32[512,1024]{0,1:T(8,128)}) %all-reduce.2.cloned.1.call-update) | async-done | bytes 2097168 | tf_op jit(solution)/shard_map/psum | solution.py:119
  (104 shorter events, 193.9 us)
Async XLA Ops:
  7.2 45.2 %all-gather.4.cloned.1.call-start = ((), (), s32[]{:S(2)}) async-start(), calls=%async_computation.1 | async-start | bytes 3145728 | tf_op jit(solution)/shard_map/all_gather | solution.py:19
  10.0 218.0 %copy-start.1 = (bf16[128,8192]{1,0:T(8,128)(2,1)S(1)}, bf16[128,8192]{1,0:T(8,128)(2,1)}, u32[]{:S(2)}) copy-start(bf16[128,8192]{1,0:T(8,128)(2,1)} %param.7) | copy-start | bytes 6291460
  10.0 218.0 %all-gather.6.cloned.1.call-start = ((), (), s32[]{:S(2)}) async-start(), calls=%async_computation.2 | async-start | bytes 18874368 | tf_op jit(solution)/shard_map/all_gather | solution.py:19
  52.4 788.0 %all-gather.8.cloned.1.call-start = ((), (), s32[]{:S(2)}) async-start(), calls=%async_computation.3 | async-start | bytes 4456448 | tf_op jit(solution)/shard_map/all_gather | solution.py:115
  236.1 26.6 %collective-permute-start = (bf16[128,1024]{1,0:T(8,128)(2,1)S(1)}, bf16[128,1024]{1,0:T(8,128)(2,1)}, u32[]{:S(2)}, u32[]{:S(2)}) collective-permute-start(bf16[128,1024]{1,0:T(8,128)(2,1)S(1)} %fusion.100), channel_id=1, source_target_pairs={{0,8},{1,9},{2,10},{3,11},{4,12},{5,13},{6,14},{7,15},{8,16},{9,17... | collective-permute-start | bytes 786440 | tf_op jit(solution)/shard_map/ppermute | solution.py:26
  240.8 28.2 %collective-permute-start.1 = (bf16[128,1024]{1,0:T(8,128)(2,1)S(1)}, bf16[128,1024]{1,0:T(8,128)(2,1)S(1)}, u32[]{:S(2)}, u32[]{:S(2)}) collective-permute-start(bf16[128,1024]{1,0:T(8,128)(2,1)S(1)} %fusion.100), channel_id=1, source_target_pairs={{0,7},{1,8},{2,9},{3,10},{4,11},{5,12},{6,13},{7,14},{8,15},{9,16}... | collective-permute-start | bytes 786440 | tf_op jit(solution)/shard_map/ppermute | solution.py:26
  245.0 45.6 %collective-permute-start.2 = (bf16[128,1024]{1,0:T(8,128)(2,1)S(1)}, bf16[128,1024]{1,0:T(8,128)(2,1)S(1)}, u32[]{:S(2)}, u32[]{:S(2)}) collective-permute-start(bf16[128,1024]{1,0:T(8,128)(2,1)S(1)} %fusion.100), channel_id=1, source_target_pairs={{0,6},{1,7},{2,8},{3,9},{4,10},{5,11},{6,12},{7,13},{8,14},{9,15},... | collective-permute-start | bytes 786440 | tf_op jit(solution)/shard_map/ppermute | solution.py:26
  255.4 50.2 %collective-permute-start.3 = (bf16[128,1024]{1,0:T(8,128)(2,1)S(1)}, bf16[128,1024]{1,0:T(8,128)(2,1)S(1)}, u32[]{:S(2)}, u32[]{:S(2)}) collective-permute-start(bf16[128,1024]{1,0:T(8,128)(2,1)S(1)} %fusion.100), channel_id=1, source_target_pairs={{0,5},{1,6},{2,7},{3,8},{4,9},{5,10},{6,11},{7,12},{8,13},{9,14},{... | collective-permute-start | bytes 786440 | tf_op jit(solution)/shard_map/ppermute | solution.py:26
  260.3 45.2 %collective-permute-start.4 = (bf16[128,1024]{1,0:T(8,128)(2,1)S(1)}, bf16[128,1024]{1,0:T(8,128)(2,1)S(1)}, u32[]{:S(2)}, u32[]{:S(2)}) collective-permute-start(bf16[128,1024]{1,0:T(8,128)(2,1)S(1)} %fusion.100), channel_id=1, source_target_pairs={{0,4},{1,5},{2,6},{3,7},{4,8},{5,9},{6,10},{7,11},{8,12},{9,13},{1... | collective-permute-start | bytes 786440 | tf_op jit(solution)/shard_map/ppermute | solution.py:26
  262.7 50.7 %collective-permute-start.5 = (bf16[128,1024]{1,0:T(8,128)(2,1)S(1)}, bf16[128,1024]{1,0:T(8,128)(2,1)S(1)}, u32[]{:S(2)}, u32[]{:S(2)}) collective-permute-start(bf16[128,1024]{1,0:T(8,128)(2,1)S(1)} %fusion.100), channel_id=1, source_target_pairs={{0,3},{1,4},{2,5},{3,6},{4,7},{5,8},{6,9},{7,10},{8,11},{9,12},{10... | collective-permute-start | bytes 786440 | tf_op jit(solution)/shard_map/ppermute | solution.py:26
  269.0 52.8 %collective-permute-start.6 = (bf16[128,1024]{1,0:T(8,128)(2,1)S(1)}, bf16[128,1024]{1,0:T(8,128)(2,1)S(1)}, u32[]{:S(2)}, u32[]{:S(2)}) collective-permute-start(bf16[128,1024]{1,0:T(8,128)(2,1)S(1)} %fusion.100), channel_id=1, source_target_pairs={{0,2},{1,3},{2,4},{3,5},{4,6},{5,7},{6,8},{7,9},{8,10},{9,11},{10,... | collective-permute-start | bytes 786440 | tf_op jit(solution)/shard_map/ppermute | solution.py:26
  290.5 43.6 %collective-permute-start.7 = (bf16[128,1024]{1,0:T(8,128)(2,1)S(1)}, bf16[128,1024]{1,0:T(8,128)(2,1)S(1)}, u32[]{:S(2)}, u32[]{:S(2)}) collective-permute-start(bf16[128,1024]{1,0:T(8,128)(2,1)S(1)} %fusion.100), channel_id=1, source_target_pairs={{0,1},{1,2},{2,3},{3,4},{4,5},{5,6},{6,7},{7,8},{8,9},{9,10},{10,1... | collective-permute-start | bytes 786440 | tf_op jit(solution)/shard_map/ppermute | solution.py:26
  516.7 127.6 %copy-start = (f32[4,1152,128]{1,2,0:T(8,128)S(1)}, f32[4,1152,128]{1,2,0:T(8,128)}, u32[]{:S(2)}) copy-start(f32[4,1152,128]{1,2,0:T(8,128)} %get-tuple-element.62) | copy-start | bytes 7077892
  518.7 18.1 %collective-permute-start.10 = (f32[128,1024]{0,1:T(8,128)S(1)}, f32[128,1024]{0,1:T(8,128)S(1)}, u32[]{:S(2)}, u32[]{:S(2)}) collective-permute-start(f32[128,1024]{0,1:T(8,128)S(1)} %get-tuple-element.156), channel_id=1, source_target_pairs={{3,0},{4,1},{5,2},{6,3},{7,4},{8,5},{9,6},{10,7},{11,8},{12,9},{13... | collective-permute-start | bytes 1572872 | tf_op jit(solution)/shard_map/ppermute | solution.py:26
  520.6 49.9 %collective-permute-start.11 = (f32[128,1024]{0,1:T(8,128)S(1)}, f32[128,1024]{0,1:T(8,128)S(1)}, u32[]{:S(2)}, u32[]{:S(2)}) collective-permute-start(f32[128,1024]{0,1:T(8,128)S(1)} %get-tuple-element.157), channel_id=1, source_target_pairs={{4,0},{5,1},{6,2},{7,3},{8,4},{9,5},{10,6},{11,7},{12,8},{13,9},{1... | collective-permute-start | bytes 1572872 | tf_op jit(solution)/shard_map/ppermute | solution.py:26
  525.2 63.1 %collective-permute-start.12 = (f32[128,1024]{0,1:T(8,128)S(1)}, f32[128,1024]{0,1:T(8,128)S(1)}, u32[]{:S(2)}, u32[]{:S(2)}) collective-permute-start(f32[128,1024]{0,1:T(8,128)S(1)} %get-tuple-element.158), channel_id=1, source_target_pairs={{5,0},{6,1},{7,2},{8,3},{9,4},{10,5},{11,6},{12,7},{13,8},{14,9},{... | collective-permute-start | bytes 1572872 | tf_op jit(solution)/shard_map/ppermute | solution.py:26
  531.0 103.8 %collective-permute-start.13 = (f32[128,1024]{0,1:T(8,128)S(1)}, f32[128,1024]{0,1:T(8,128)S(1)}, u32[]{:S(2)}, u32[]{:S(2)}) collective-permute-start(f32[128,1024]{0,1:T(8,128)S(1)} %get-tuple-element.159), channel_id=1, source_target_pairs={{6,0},{7,1},{8,2},{9,3},{10,4},{11,5},{12,6},{13,7},{14,8},{15,9},... | collective-permute-start | bytes 1572872 | tf_op jit(solution)/shard_map/ppermute | solution.py:26
  533.0 109.3 %collective-permute-start.14 = (f32[128,1024]{0,1:T(8,128)S(1)}, f32[128,1024]{0,1:T(8,128)S(1)}, u32[]{:S(2)}, u32[]{:S(2)}) collective-permute-start(f32[128,1024]{0,1:T(8,128)S(1)} %get-tuple-element.161), channel_id=1, source_target_pairs={{7,0},{8,1},{9,2},{10,3},{11,4},{12,5},{13,6},{14,7},{15,8},{16,9}... | collective-permute-start | bytes 1572872 | tf_op jit(solution)/shard_map/ppermute | solution.py:26
  536.8 105.5 %collective-permute-start.15 = (f32[128,1024]{0,1:T(8,128)S(1)}, f32[128,1024]{0,1:T(8,128)S(1)}, u32[]{:S(2)}, u32[]{:S(2)}) collective-permute-start(f32[128,1024]{0,1:T(8,128)S(1)} %get-tuple-element.160), channel_id=1, source_target_pairs={{8,0},{9,1},{10,2},{11,3},{12,4},{13,5},{14,6},{15,7},{16,8},{17,9... | collective-permute-start | bytes 1572872 | tf_op jit(solution)/shard_map/ppermute | solution.py:26
  570.5 71.8 %collective-permute-start.8 = (f32[128,1024]{0,1:T(8,128)S(1)}, f32[128,1024]{0,1:T(8,128)S(1)}, u32[]{:S(2)}, u32[]{:S(2)}) collective-permute-start(f32[128,1024]{0,1:T(8,128)S(1)} %get-tuple-element.154), channel_id=1, source_target_pairs={{1,0},{2,1},{3,2},{4,3},{5,4},{6,5},{7,6},{8,7},{9,8},{10,9},{11,1... | collective-permute-start | bytes 1572872 | tf_op jit(solution)/shard_map/ppermute | solution.py:26
  588.3 54.0 %copy-start.2 = (f32[128,1024]{0,1:T(8,128)}, f32[128,1024]{0,1:T(8,128)S(1)}, u32[]{:S(2)}) copy-start(f32[128,1024]{0,1:T(8,128)S(1)} %collective-permute-done.12) | copy-start | bytes 1572868
  588.3 54.0 %collective-permute-start.9 = (f32[128,1024]{0,1:T(8,128)S(1)}, f32[128,1024]{0,1:T(8,128)S(1)}, u32[]{:S(2)}, u32[]{:S(2)}) collective-permute-start(f32[128,1024]{0,1:T(8,128)S(1)} %get-tuple-element.155), channel_id=1, source_target_pairs={{2,0},{3,1},{4,2},{5,3},{6,4},{7,5},{8,6},{9,7},{10,8},{11,9},{12,... | collective-permute-start | bytes 1572872 | tf_op jit(solution)/shard_map/ppermute | solution.py:26
  634.7 7.6 copy-start.3
  645.4 357.4 %all-reduce.2.cloned.1.call-start = ((), (), s32[]{:S(2)}) async-start(), calls=%async_computation.4 | async-start | bytes 4194304 | tf_op jit(solution)/shard_map/psum | solution.py:119
  (6 other events, 8.4 us)
Sparse Core Ops, SparseCore 0:
  10.4 41.9 all-gather.3
  54.2 173.7 all-gather.5
  645.5 194.9 all-gather.7
  847.1 155.5 all-reduce.1
where the time goes:
time: 1010 us
  waiting for transfers between devices  529 us (52%)
  matrix products  206 us (20%)
  blocking collectives  131 us (13%)
  starting transfers between devices  97.6 us (10%)
  local copies, waits for them, and re-layouts  27.1 us (3%)
  between operations  14.2 us (1%)
    all_gather x2, waiting for transfers between devices, gather_axes(): nearer = lax.all_gather(value, axes[-1], axis=dim, tiled=True)  218 us
    psum x1, waiting for transfers between devices, body(): weight_grad = lax.psum(shard_grad, 'seq')  136 us
    all_to_all x1, blocking collectives, body(): lax.all_to_all(hidden, FSDP, split_axis=1, concat_axis=0, tiled=True)  131 us
    ppermute x16, waiting for transfers between devices, shifted(): return lax.ppermute(block, axis, route)  118 us
    ppermute x16, starting transfers between devices, shifted(): return lax.ppermute(block, axis, route)  97.5 us
    all_gather x1, waiting for transfers between devices, body(): lax.all_gather(all_grad, FSDP, axis=0, tiled=True)  56 us
    dot_general x4, matrix products, attend_group(): jnp.einsum('rhk,kd->rhd', dscores, kgrp, preferred_element_type=jnp.float32)  50.1 us
    dot_general x4, matrix products, attend_group(): jnp.einsum('rhk,rhd->kd', dscores, qgrp, preferred_element_type=jnp.float32)  48.3 us
  transfers between devices with their start and end apart: 20, of which 13 were waited for; matrix products, arithmetic and copies ran while one was open for 3% of the time, Pallas kernels for 0%

commit v1 on v0

--- a/solution.py
+++ b/solution.py
@@ -75,6 +75,13 @@
 
 
 def body(hidden, kv_blocks, kv_scale, queries, grad_out):
+
+    def loops_save(array_in):
+        found_now = jnp.concatenate(
+            jax.lax.all_to_all(jnp.stack([array_in] * jax.lax.psum(1, FSDP)), FSDP, 0, 0), axis=0
+        )
+        return found_now
+
     tok = hidden.shape[0]
     groups = lax.axis_size(FSDP)
     reach = groups // 2
@@ -111,10 +118,7 @@
         seg_grad, whole, (((1,), (1,)), ((), ())), preferred_element_type=jnp.float32
     ).astype(jnp.bfloat16)
     shard_grad = lax.dot_general(
-        columns,
-        lax.all_gather(all_grad, FSDP, axis=0, tiled=True),
-        (((0,), (0,)), ((), ())),
-        preferred_element_type=jnp.float32,
+        columns, loops_save(all_grad), (((0,), (0,)), ((), ())), preferred_element_type=jnp.float32
     )
     weight_grad = lax.psum(shard_grad, "seq")
     return (attn_out, grad_queries, grad_hidden, weight_grad)

time: 1010 us -> 1010 us (level)
  waiting for transfers between devices: 529 us -> 492 us
  blocking collectives: 131 us -> 163 us
    all_gather x1 -> x0, waiting for transfers between devices: 56 us -> none  [body(): lax.all_gather(all_grad, FSDP, axis=0, tiled=True)]
    all_to_all x1, blocking collectives: 131 us -> 163 us  [loops_save(): jax.lax.all_to_all(jnp.stack([array_in] * jax.lax.psum(1, FSDP)), FSDP, 0...]
    all_gather x2, waiting for transfers between devices: 218 us -> 249 us  [gather_axes(): nearer = lax.all_gather(value, axes[-1], axis=dim, tiled=True)]
    psum x1, waiting for transfers between devices: 136 us -> 125 us  [body(): weight_grad = lax.psum(shard_grad, 'seq')]
  transfers between devices with their start and end apart: 20 -> 20, of which waited for: 13 -> 12; matrix products, arithmetic and copies ran while one was open for 3% -> 22% of each run, Pallas kernels for 0% -> 0%
where the time goes in v1:
time: 1010 us
  waiting for transfers between devices  492 us (49%)
  matrix products  205 us (20%)
  blocking collectives  163 us (16%)
  starting transfers between devices  104 us (10%)
  local copies, waits for them, and re-layouts  27.1 us (3%)
  between operations  14.2 us (1%)
    all_gather x2, waiting for transfers between devices, gather_axes(): nearer = lax.all_gather(value, axes[-1], axis=dim, tiled=True)  249 us
    all_to_all x1, blocking collectives, loops_save(): jax.lax.all_to_all(jnp.stack([array_in] * jax.lax.psum(1, FSDP)), FSDP, 0...  163 us
    psum x1, waiting for transfers between devices, body(): weight_grad = lax.psum(shard_grad, 'seq')  125 us
    ppermute x16, waiting for transfers between devices, shifted(): return lax.ppermute(block, axis, route)  119 us
    ppermute x16, starting transfers between devices, shifted(): return lax.ppermute(block, axis, route)  97.1 us
    dot_general x4, matrix products, attend_group(): jnp.einsum('rhk,kd->rhd', dscores, kgrp, preferred_element_type=jnp.float32)  50.4 us
    dot_general x4, matrix products, attend_group(): jnp.einsum('rhk,rhd->kd', dscores, qgrp, preferred_element_type=jnp.float32)  48.5 us
    sub x4, matrix products, attend_group(): expd = jnp.exp(scores - top)  23 us
  transfers between devices with their start and end apart: 20, of which 12 were waited for; matrix products, arithmetic and copies ran while one was open for 22% of the time, Pallas kernels for 0%

profile of v1, /device:TPU:1, one launch (start us, length us, event | category | flops | bytes accessed | tf_op | source)
XLA Modules:
  0.0 1013.3 jit_solution(11100136131444230876)
XLA Ops:
  10.0 42.4 %all-gather.3.cloned.1.call-done = bf16[1024,1024]{1,0:T(8,128)(2,1)} async-done(((bf16[512,1024]{1,0:T(8,128)(2,1)}), bf16[1024,1024]{1,0:T(8,128)(2,1)}) %all-gather.3.cloned.1.call-update) | async-done | bytes 2097168 | tf_op jit(solution)/shard_map/all_gather | solution.py:19
  65.8 206.7 %all-gather.5.cloned.1.call-done = bf16[8192,1024]{1,0:T(8,128)(2,1)} async-done(((bf16[1024,1024]{1,0:T(8,128)(2,1)}), bf16[8192,1024]{1,0:T(8,128)(2,1)}) %all-gather.5.cloned.1.call-update) | async-done | bytes 16777232 | tf_op jit(solution)/shard_map/all_gather | solution.py:19
  272.4 8.1 fusion.105
  316.5 18.6 %collective-permute-done.2 = bf16[128,1024]{1,0:T(8,128)(2,1)S(1)} collective-permute-done((bf16[128,1024]{1,0:T(8,128)(2,1)S(1)}, bf16[128,1024]{1,0:T(8,128)(2,1)S(1)}, u32[]{:S(2)}, u32[]{:S(2)}) %collective-permute-start.2) | collective-permute-done | bytes 262176 | tf_op jit(solution)/shard_map/ppermute | solution.py:26
  337.0 15.4 %collective-permute-done.3 = bf16[128,1024]{1,0:T(8,128)(2,1)S(1)} collective-permute-done((bf16[128,1024]{1,0:T(8,128)(2,1)S(1)}, bf16[128,1024]{1,0:T(8,128)(2,1)S(1)}, u32[]{:S(2)}, u32[]{:S(2)}) %collective-permute-start.3) | collective-permute-done | bytes 262176 | tf_op jit(solution)/shard_map/ppermute | solution.py:26
  358.3 8.3 collective-permute-done.6
  366.6 12.2 %collective-permute-done.7 = bf16[128,1024]{1,0:T(8,128)(2,1)S(1)} collective-permute-done((bf16[128,1024]{1,0:T(8,128)(2,1)S(1)}, bf16[128,1024]{1,0:T(8,128)(2,1)S(1)}, u32[]{:S(2)}, u32[]{:S(2)}) %collective-permute-start.7) | collective-permute-done | bytes 262176 | tf_op jit(solution)/shard_map/ppermute | solution.py:26
  380.8 181.1 %while.17 = (s32[]{:T(128)}, bf16[4,128,8,128]{3,1,2,0:T(8,128)(2,1)}, bf16[4,128,8,128]{3,1,2,0:T(8,128)(2,1)}, f32[4,1152,128]{1,2,0:T(8,128)S(1)}, f32[4,1152...) while((s32[]{:T(128)}, ...), condition=%wide.region_4.5_spmd.clone, body=%wide.region_0.4_spmd.clone.sunk | while | flops 2449958400 | bytes 52865276 | solution.py:67
  391.4 12.1 %fusion.175 = f32[4,1152,128]{1,2,0:T(8,128)S(1)} fusion(f32[4,1152,128]{1,2,0:T(8,128)S(1)} %get-tuple-element.243, s32[]{:T(128)} %get-tuple-element.240, f32[128,8,1152]{2,0,1:T(8,128)} %fusion.173, bf16[4,128,8,128]{1,3,2,0:T(8,128)(2,1)} %get-tuple-element.258, f32[128,8,1152]{2,0,1:T(8,128)} %get-tuple-element.226, ...), kind=kOutput, calls=%fused_computation.17.clone.1 | convolution fusion | flops 310249600 | bytes 19735552 | tf_op jit(solution)/shard_map/while/body/eval_jaxpr/rhk,rhd->kd/dot_general | solution.py:53
  403.5 12.6 %fusion.174 = bf16[4,128,8,128]{3,1,2,0:T(8,128)(2,1)} fusion(bf16[4,128,8,128]{3,1,2,0:T(8,128)(2,1)} %get-tuple-element.242, s32[]{:T(128)} %get-tuple-element.240, f32[128,8,1152]{2,0,1:T(8,128)} %fusion.173, bf16[4,1152,128]{2,1,0:T(8,128)(2,1)} %get-tuple-element.259, f32[128,8,1152]{2,0,1:T(8,128)} %get-tuple-element.226, ...), kind=kOutput, calls=%fused_computation.28.clone.1 | convolution fusion | flops 310380672 | bytes 19440640 | tf_op jit(solution)/shard_map/while/body/eval_jaxpr/rhk,kd->rhd/dot_general | solution.py:50
  436.7 12.1 %fusion.175 = f32[4,1152,128]{1,2,0:T(8,128)S(1)} fusion(f32[4,1152,128]{1,2,0:T(8,128)S(1)} %get-tuple-element.243, s32[]{:T(128)} %get-tuple-element.240, f32[128,8,1152]{2,0,1:T(8,128)} %fusion.173, bf16[4,128,8,128]{1,3,2,0:T(8,128)(2,1)} %get-tuple-element.258, f32[128,8,1152]{2,0,1:T(8,128)} %get-tuple-element.226, ...), kind=kOutput, calls=%fused_computation.17.clone.1 | convolution fusion | flops 310249600 | bytes 19735552 | tf_op jit(solution)/shard_map/while/body/eval_jaxpr/rhk,rhd->kd/dot_general | solution.py:53
  448.8 12.6 %fusion.174 = bf16[4,128,8,128]{3,1,2,0:T(8,128)(2,1)} fusion(bf16[4,128,8,128]{3,1,2,0:T(8,128)(2,1)} %get-tuple-element.242, s32[]{:T(128)} %get-tuple-element.240, f32[128,8,1152]{2,0,1:T(8,128)} %fusion.173, bf16[4,1152,128]{2,1,0:T(8,128)(2,1)} %get-tuple-element.259, f32[128,8,1152]{2,0,1:T(8,128)} %get-tuple-element.226, ...), kind=kOutput, calls=%fused_computation.28.clone.1 | convolution fusion | flops 310380672 | bytes 19440640 | tf_op jit(solution)/shard_map/while/body/eval_jaxpr/rhk,kd->rhd/dot_general | solution.py:50
  482.0 12.1 %fusion.175 = f32[4,1152,128]{1,2,0:T(8,128)S(1)} fusion(f32[4,1152,128]{1,2,0:T(8,128)S(1)} %get-tuple-element.243, s32[]{:T(128)} %get-tuple-element.240, f32[128,8,1152]{2,0,1:T(8,128)} %fusion.173, bf16[4,128,8,128]{1,3,2,0:T(8,128)(2,1)} %get-tuple-element.258, f32[128,8,1152]{2,0,1:T(8,128)} %get-tuple-element.226, ...), kind=kOutput, calls=%fused_computation.17.clone.1 | convolution fusion | flops 310249600 | bytes 19735552 | tf_op jit(solution)/shard_map/while/body/eval_jaxpr/rhk,rhd->kd/dot_general | solution.py:53
  494.1 12.6 %fusion.174 = bf16[4,128,8,128]{3,1,2,0:T(8,128)(2,1)} fusion(bf16[4,128,8,128]{3,1,2,0:T(8,128)(2,1)} %get-tuple-element.242, s32[]{:T(128)} %get-tuple-element.240, f32[128,8,1152]{2,0,1:T(8,128)} %fusion.173, bf16[4,1152,128]{2,1,0:T(8,128)(2,1)} %get-tuple-element.259, f32[128,8,1152]{2,0,1:T(8,128)} %get-tuple-element.226, ...), kind=kOutput, calls=%fused_computation.28.clone.1 | convolution fusion | flops 310380672 | bytes 19440640 | tf_op jit(solution)/shard_map/while/body/eval_jaxpr/rhk,kd->rhd/dot_general | solution.py:50
  527.3 12.1 %fusion.175 = f32[4,1152,128]{1,2,0:T(8,128)S(1)} fusion(f32[4,1152,128]{1,2,0:T(8,128)S(1)} %get-tuple-element.243, s32[]{:T(128)} %get-tuple-element.240, f32[128,8,1152]{2,0,1:T(8,128)} %fusion.173, bf16[4,128,8,128]{1,3,2,0:T(8,128)(2,1)} %get-tuple-element.258, f32[128,8,1152]{2,0,1:T(8,128)} %get-tuple-element.226, ...), kind=kOutput, calls=%fused_computation.17.clone.1 | convolution fusion | flops 310249600 | bytes 19735552 | tf_op jit(solution)/shard_map/while/body/eval_jaxpr/rhk,rhd->kd/dot_general | solution.py:53
  539.4 12.6 %fusion.174 = bf16[4,128,8,128]{3,1,2,0:T(8,128)(2,1)} fusion(bf16[4,128,8,128]{3,1,2,0:T(8,128)(2,1)} %get-tuple-element.242, s32[]{:T(128)} %get-tuple-element.240, f32[128,8,1152]{2,0,1:T(8,128)} %fusion.173, bf16[4,1152,128]{2,1,0:T(8,128)(2,1)} %get-tuple-element.259, f32[128,8,1152]{2,0,1:T(8,128)} %get-tuple-element.226, ...), kind=kOutput, calls=%fused_computation.28.clone.1 | convolution fusion | flops 310380672 | bytes 19440640 | tf_op jit(solution)/shard_map/while/body/eval_jaxpr/rhk,kd->rhd/dot_general | solution.py:50
  582.0 17.8 %collective-permute-start.15 = (f32[128,1024]{0,1:T(8,128)S(1)}, f32[128,1024]{0,1:T(8,128)S(1)}, u32[]{:S(2)}, u32[]{:S(2)}) collective-permute-start(f32[128,1024]{0,1:T(8,128)S(1)} %get-tuple-element.144), channel_id=1, source_target_pairs={{8,0},{9,1},{10,2},{11,3},{12,4},{13,5},{14,6},{15,7},{16,8},{17,9... | collective-permute-start | bytes 1572872 | tf_op jit(solution)/shard_map/ppermute | solution.py:26
  599.8 16.0 %collective-permute-done.11 = f32[128,1024]{0,1:T(8,128)S(1)} collective-permute-done((f32[128,1024]{0,1:T(8,128)S(1)}, f32[128,1024]{0,1:T(8,128)S(1)}, u32[]{:S(2)}, u32[]{:S(2)}) %collective-permute-start.11) | collective-permute-done | bytes 524320 | tf_op jit(solution)/shard_map/ppermute | solution.py:26
  615.8 17.9 %collective-permute-start.8 = (f32[128,1024]{0,1:T(8,128)S(1)}, f32[128,1024]{0,1:T(8,128)S(1)}, u32[]{:S(2)}, u32[]{:S(2)}) collective-permute-start(f32[128,1024]{0,1:T(8,128)S(1)} %get-tuple-element.138), channel_id=1, source_target_pairs={{1,0},{2,1},{3,2},{4,3},{5,4},{6,5},{7,6},{8,7},{9,8},{10,9},{11,1... | collective-permute-start | bytes 1572872 | tf_op jit(solution)/shard_map/ppermute | solution.py:26
  633.7 13.1 %collective-permute-start.9 = (f32[128,1024]{0,1:T(8,128)S(1)}, f32[128,1024]{0,1:T(8,128)S(1)}, u32[]{:S(2)}, u32[]{:S(2)}) collective-permute-start(f32[128,1024]{0,1:T(8,128)S(1)} %get-tuple-element.139), channel_id=1, source_target_pairs={{2,0},{3,1},{4,2},{5,3},{6,4},{7,5},{8,6},{9,7},{10,8},{11,9},{12,... | collective-permute-start | bytes 1572872 | tf_op jit(solution)/shard_map/ppermute | solution.py:26
  646.8 32.7 %collective-permute-done.13 = f32[128,1024]{0,1:T(8,128)S(1)} collective-permute-done((f32[128,1024]{0,1:T(8,128)S(1)}, f32[128,1024]{0,1:T(8,128)S(1)}, u32[]{:S(2)}, u32[]{:S(2)}) %collective-permute-start.13) | collective-permute-done | bytes 524320 | tf_op jit(solution)/shard_map/ppermute | solution.py:26
  691.9 162.5 %all_to_all.21 = bf16[16,128,1024]{1,2,0:T(8,128)(2,1)S(1)} all-to-all(bf16[16,128,1024]{1,2,0:T(8,128)(2,1)S(1)} %stack.2), channel_id=1, replica_groups=mesh['seq'=16,'fsdp_0'=8,'fsdp_1'=2] {'fsdp_0','fsdp_1'}, dimensions={0} | all-to-all | bytes 8388608 | tf_op jit(solution)/shard_map/all_to_all | solution.py:81
  865.3 14.1 %convolution_convert_fusion.1 = bf16[128,8192]{1,0:T(8,128)(2,1)} fusion(bf16[8192,1024]{1,0:T(8,128)(2,1)} %all-gather.5.cloned.1.call-done, f32[128,1024]{0,1:T(8,128)} %copy-done.5, f32[128,1024]{0,1:T(8,128)} %copy-done.4, f32[128,1024]{0,1:T(8,128)} %copy-done.3, f32[128,1024]{0,1:T(8,128)} %copy-done.2, f32[128,1024]{0,1:T(8,128)S(1)} %collective-permute-done.11, ...), kind=kOutput, calls=%fused_computation.83 | convolution fusion | flops 2150891520 | bytes 27787272 | tf_op jit(solution)/shard_map/dot_general | solution.py:117
  879.3 124.5 %all-reduce.2.cloned.1.call-done = f32[512,1024]{0,1:T(8,128)} async-done(((f32[512,1024]{0,1:T(8,128)}), f32[512,1024]{0,1:T(8,128)}) %all-reduce.2.cloned.1.call-update) | async-done | bytes 2097168 | tf_op jit(solution)/shard_map/psum | solution.py:123
  (104 shorter events, 189.8 us)
Async XLA Ops:
  7.2 45.2 %all-gather.3.cloned.1.call-start = ((), (), s32[]{:S(2)}) async-start(), calls=%async_computation.2 | async-start | bytes 3145728 | tf_op jit(solution)/shard_map/all_gather | solution.py:19
  10.0 42.5 %copy-start.1 = (bf16[128,8192]{1,0:T(8,128)(2,1)S(1)}, bf16[128,8192]{1,0:T(8,128)(2,1)}, u32[]{:S(2)}) copy-start(bf16[128,8192]{1,0:T(8,128)(2,1)} %param.7) | copy-start | bytes 6291460
  10.0 262.5 %all-gather.5.cloned.1.call-start = ((), (), s32[]{:S(2)}) async-start(), calls=%async_computation.3 | async-start | bytes 18874368 | tf_op jit(solution)/shard_map/all_gather | solution.py:19
  58.8 631.4 %all-to-all-start.1 = ((bf16[128,16,512]{2,0,1:T(8,128)(2,1)}), bf16[128,16,512]{2,0,1:T(8,128)(2,1)}, u32[]{:S(2)}, u32[]{:S(2)}) async-start(bf16[128,16,512]{2,0,1:T(8,128)(2,1)} %copy.29), calls=%async_computation.1 | async-start | bytes 4194304 | tf_op jit(solution)/shard_map/all_to_all | solution.py:91
  65.7 938.2 %all-reduce.2.cloned.1.call-start = ((), (), s32[]{:S(2)}) async-start(), calls=%async_computation.4 | async-start | bytes 4194304 | tf_op jit(solution)/shard_map/psum | solution.py:123
  280.6 26.5 %collective-permute-start = (bf16[128,1024]{1,0:T(8,128)(2,1)S(1)}, bf16[128,1024]{1,0:T(8,128)(2,1)}, u32[]{:S(2)}, u32[]{:S(2)}) collective-permute-start(bf16[128,1024]{1,0:T(8,128)(2,1)S(1)} %fusion.105), channel_id=1, source_target_pairs={{0,8},{1,9},{2,10},{3,11},{4,12},{5,13},{6,14},{7,15},{8,16},{9,17... | collective-permute-start | bytes 786440 | tf_op jit(solution)/shard_map/ppermute | solution.py:26
  285.5 28.2 %collective-permute-start.1 = (bf16[128,1024]{1,0:T(8,128)(2,1)S(1)}, bf16[128,1024]{1,0:T(8,128)(2,1)S(1)}, u32[]{:S(2)}, u32[]{:S(2)}) collective-permute-start(bf16[128,1024]{1,0:T(8,128)(2,1)S(1)} %fusion.105), channel_id=1, source_target_pairs={{0,7},{1,8},{2,9},{3,10},{4,11},{5,12},{6,13},{7,14},{8,15},{9,16}... | collective-permute-start | bytes 786440 | tf_op jit(solution)/shard_map/ppermute | solution.py:26
  289.5 45.6 %collective-permute-start.2 = (bf16[128,1024]{1,0:T(8,128)(2,1)S(1)}, bf16[128,1024]{1,0:T(8,128)(2,1)S(1)}, u32[]{:S(2)}, u32[]{:S(2)}) collective-permute-start(bf16[128,1024]{1,0:T(8,128)(2,1)S(1)} %fusion.105), channel_id=1, source_target_pairs={{0,6},{1,7},{2,8},{3,9},{4,10},{5,11},{6,12},{7,13},{8,14},{9,15},... | collective-permute-start | bytes 786440 | tf_op jit(solution)/shard_map/ppermute | solution.py:26
  300.2 52.2 %collective-permute-start.3 = (bf16[128,1024]{1,0:T(8,128)(2,1)S(1)}, bf16[128,1024]{1,0:T(8,128)(2,1)S(1)}, u32[]{:S(2)}, u32[]{:S(2)}) collective-permute-start(bf16[128,1024]{1,0:T(8,128)(2,1)S(1)} %fusion.105), channel_id=1, source_target_pairs={{0,5},{1,6},{2,7},{3,8},{4,9},{5,10},{6,11},{7,12},{8,13},{9,14},{... | collective-permute-start | bytes 786440 | tf_op jit(solution)/shard_map/ppermute | solution.py:26
  304.8 47.6 %collective-permute-start.4 = (bf16[128,1024]{1,0:T(8,128)(2,1)S(1)}, bf16[128,1024]{1,0:T(8,128)(2,1)S(1)}, u32[]{:S(2)}, u32[]{:S(2)}) collective-permute-start(bf16[128,1024]{1,0:T(8,128)(2,1)S(1)} %fusion.105), channel_id=1, source_target_pairs={{0,4},{1,5},{2,6},{3,7},{4,8},{5,9},{6,10},{7,11},{8,12},{9,13},{1... | collective-permute-start | bytes 786440 | tf_op jit(solution)/shard_map/ppermute | solution.py:26
  307.0 51.3 %collective-permute-start.5 = (bf16[128,1024]{1,0:T(8,128)(2,1)S(1)}, bf16[128,1024]{1,0:T(8,128)(2,1)S(1)}, u32[]{:S(2)}, u32[]{:S(2)}) collective-permute-start(bf16[128,1024]{1,0:T(8,128)(2,1)S(1)} %fusion.105), channel_id=1, source_target_pairs={{0,3},{1,4},{2,5},{3,6},{4,7},{5,8},{6,9},{7,10},{8,11},{9,12},{10... | collective-permute-start | bytes 786440 | tf_op jit(solution)/shard_map/ppermute | solution.py:26
  313.7 52.9 %collective-permute-start.6 = (bf16[128,1024]{1,0:T(8,128)(2,1)S(1)}, bf16[128,1024]{1,0:T(8,128)(2,1)S(1)}, u32[]{:S(2)}, u32[]{:S(2)}) collective-permute-start(bf16[128,1024]{1,0:T(8,128)(2,1)S(1)} %fusion.105), channel_id=1, source_target_pairs={{0,2},{1,3},{2,4},{3,5},{4,6},{5,7},{6,8},{7,9},{8,10},{9,11},{10,... | collective-permute-start | bytes 786440 | tf_op jit(solution)/shard_map/ppermute | solution.py:26
  335.1 43.8 %collective-permute-start.7 = (bf16[128,1024]{1,0:T(8,128)(2,1)S(1)}, bf16[128,1024]{1,0:T(8,128)(2,1)S(1)}, u32[]{:S(2)}, u32[]{:S(2)}) collective-permute-start(bf16[128,1024]{1,0:T(8,128)(2,1)S(1)} %fusion.105), channel_id=1, source_target_pairs={{0,1},{1,2},{2,3},{3,4},{4,5},{5,6},{6,7},{7,8},{8,9},{9,10},{10,1... | collective-permute-start | bytes 786440 | tf_op jit(solution)/shard_map/ppermute | solution.py:26
  561.9 127.1 %copy-start = (f32[4,1152,128]{1,2,0:T(8,128)S(1)}, f32[4,1152,128]{1,2,0:T(8,128)}, u32[]{:S(2)}) copy-start(f32[4,1152,128]{1,2,0:T(8,128)} %get-tuple-element.62) | copy-start | bytes 7077892
  563.9 18.1 %collective-permute-start.10 = (f32[128,1024]{0,1:T(8,128)S(1)}, f32[128,1024]{0,1:T(8,128)S(1)}, u32[]{:S(2)}, u32[]{:S(2)}) collective-permute-start(f32[128,1024]{0,1:T(8,128)S(1)} %get-tuple-element.140), channel_id=1, source_target_pairs={{3,0},{4,1},{5,2},{6,3},{7,4},{8,5},{9,6},{10,7},{11,8},{12,9},{13... | collective-permute-start | bytes 1572872 | tf_op jit(solution)/shard_map/ppermute | solution.py:26
  565.8 50.0 %collective-permute-start.11 = (f32[128,1024]{0,1:T(8,128)S(1)}, f32[128,1024]{0,1:T(8,128)S(1)}, u32[]{:S(2)}, u32[]{:S(2)}) collective-permute-start(f32[128,1024]{0,1:T(8,128)S(1)} %get-tuple-element.141), channel_id=1, source_target_pairs={{4,0},{5,1},{6,2},{7,3},{8,4},{9,5},{10,6},{11,7},{12,8},{13,9},{1... | collective-permute-start | bytes 1572872 | tf_op jit(solution)/shard_map/ppermute | solution.py:26
  570.1 63.6 %collective-permute-start.12 = (f32[128,1024]{0,1:T(8,128)S(1)}, f32[128,1024]{0,1:T(8,128)S(1)}, u32[]{:S(2)}, u32[]{:S(2)}) collective-permute-start(f32[128,1024]{0,1:T(8,128)S(1)} %get-tuple-element.142), channel_id=1, source_target_pairs={{5,0},{6,1},{7,2},{8,3},{9,4},{10,5},{11,6},{12,7},{13,8},{14,9},{... | collective-permute-start | bytes 1572872 | tf_op jit(solution)/shard_map/ppermute | solution.py:26
  576.1 103.4 %collective-permute-start.13 = (f32[128,1024]{0,1:T(8,128)S(1)}, f32[128,1024]{0,1:T(8,128)S(1)}, u32[]{:S(2)}, u32[]{:S(2)}) collective-permute-start(f32[128,1024]{0,1:T(8,128)S(1)} %get-tuple-element.143), channel_id=1, source_target_pairs={{6,0},{7,1},{8,2},{9,3},{10,4},{11,5},{12,6},{13,7},{14,8},{15,9},... | collective-permute-start | bytes 1572872 | tf_op jit(solution)/shard_map/ppermute | solution.py:26
  578.1 109.0 %collective-permute-start.14 = (f32[128,1024]{0,1:T(8,128)S(1)}, f32[128,1024]{0,1:T(8,128)S(1)}, u32[]{:S(2)}, u32[]{:S(2)}) collective-permute-start(f32[128,1024]{0,1:T(8,128)S(1)} %get-tuple-element.145), channel_id=1, source_target_pairs={{7,0},{8,1},{9,2},{10,3},{11,4},{12,5},{13,6},{14,7},{15,8},{16,9}... | collective-permute-start | bytes 1572872 | tf_op jit(solution)/shard_map/ppermute | solution.py:26
  582.0 105.2 %collective-permute-start.15 = (f32[128,1024]{0,1:T(8,128)S(1)}, f32[128,1024]{0,1:T(8,128)S(1)}, u32[]{:S(2)}, u32[]{:S(2)}) collective-permute-start(f32[128,1024]{0,1:T(8,128)S(1)} %get-tuple-element.144), channel_id=1, source_target_pairs={{8,0},{9,1},{10,2},{11,3},{12,4},{13,5},{14,6},{15,7},{16,8},{17,9... | collective-permute-start | bytes 1572872 | tf_op jit(solution)/shard_map/ppermute | solution.py:26
  615.8 71.4 %collective-permute-start.8 = (f32[128,1024]{0,1:T(8,128)S(1)}, f32[128,1024]{0,1:T(8,128)S(1)}, u32[]{:S(2)}, u32[]{:S(2)}) collective-permute-start(f32[128,1024]{0,1:T(8,128)S(1)} %get-tuple-element.138), channel_id=1, source_target_pairs={{1,0},{2,1},{3,2},{4,3},{5,4},{6,5},{7,6},{8,7},{9,8},{10,9},{11,1... | collective-permute-start | bytes 1572872 | tf_op jit(solution)/shard_map/ppermute | solution.py:26
  633.7 53.5 %copy-start.2 = (f32[128,1024]{0,1:T(8,128)}, f32[128,1024]{0,1:T(8,128)S(1)}, u32[]{:S(2)}) copy-start(f32[128,1024]{0,1:T(8,128)S(1)} %collective-permute-done.12) | copy-start | bytes 1572868
  633.7 53.5 %collective-permute-start.9 = (f32[128,1024]{0,1:T(8,128)S(1)}, f32[128,1024]{0,1:T(8,128)S(1)}, u32[]{:S(2)}, u32[]{:S(2)}) collective-permute-start(f32[128,1024]{0,1:T(8,128)S(1)} %get-tuple-element.139), channel_id=1, source_target_pairs={{2,0},{3,1},{4,2},{5,3},{6,4},{7,5},{8,6},{9,7},{10,8},{11,9},{12,... | collective-permute-start | bytes 1572872 | tf_op jit(solution)/shard_map/ppermute | solution.py:26
  679.6 7.6 copy-start.3
  (6 other events, 8.3 us)
Sparse Core Ops, SparseCore 0:
  10.4 41.9 all-gather.2
  54.2 218.1 all-gather.4
  859.8 143.9 all-reduce.1
